TPU v7x, 32 devices: a whole 2x2x4 slice. The times are simulated.
32 devices in a mesh: expert: 8 (over z, x), tensor: 4 (over y, core).
Axes of the slice: x: 2, y: 2, z: 4, core: 2. Of those that a mesh axis runs over, the one named last changes fastest.
Arguments:
- tokens: bfloat16 [512, 8192], P('expert', 'tensor'), may hold values from -6 to 6
- frozen_gate_weight: bfloat16 [8192, 28672], P('tensor', 'expert'), may hold values from -0.0625 to 0.0625
- frozen_up_weight: bfloat16 [8192, 28672], P('tensor', 'expert'), may hold values from -0.0625 to 0.0625
- frozen_down_weight: bfloat16 [28672, 8192], P('expert', 'tensor'), may hold values from -0.03125 to 0.03125
- adapter_down_weight: bfloat16 [32, 8192, 128], P('expert', 'tensor'), may hold values from -0.0625 to 0.0625
- adapter_up_weight: bfloat16 [32, 128, 8192], P('expert', None, 'tensor'), may hold values from -0.0625 to 0.0625
- routes: int32 [512, 2], P('expert'), may hold values from 0 to 31, all different within a row; in each aligned block of 64 rows (0 to 63, 64 to 127, ...) at most 8 rows name the same one
- route_gate_weights: float32 [512, 2], P('expert'), may hold values from 0.1 to 1
- output_gradient: bfloat16 [512, 8192], P('expert', 'tensor'), may hold values from -6 to 6
Outputs:
- ffn_out: bfloat16 [512, 8192], P('expert', 'tensor')
- grad_down: bfloat16 [32, 8192, 128], P('expert', 'tensor')
- grad_up: bfloat16 [32, 128, 8192], P('expert', None, 'tensor')
Inputs may be any that keep to these rules, and one draw needn't show every extreme that they name: `routes`: the two experts of a token differ. Among the 64 rows of one index of expert no expert is named more than 8 times, and in some such rows one expert is named exactly 8 times.
All inputs are finite; a program needn't handle non-finite values.
Results may differ from a plain program's by a relative error of at most 0.025.
Values may be sent and summed in bfloat16 or wider, within the bound.
A program may use at most 128 MiB of HBM per device.

v0:
```python
import jax
import jax.numpy as jnp
from jax import lax
from jax.sharding import PartitionSpec as P

F32 = jnp.float32
BF16 = jnp.bfloat16


def activate(gate_part, up_part):
    return (jax.nn.silu(gate_part) * up_part).astype(BF16)


def frozen_layer(shard_rows, gate_weight, up_weight, down_weight):
    hidden_width = gate_weight.shape[1]
    gate_part = jnp.dot(shard_rows, gate_weight, preferred_element_type=F32).astype(BF16)
    up_part = jnp.dot(shard_rows, up_weight, preferred_element_type=F32).astype(BF16)
    summed = lax.psum_scatter(
        jnp.concatenate([gate_part, up_part], axis=1), "tensor", scatter_dimension=0, tiled=True
    ).astype(F32)
    hidden = activate(summed[:, :hidden_width], summed[:, hidden_width:])
    hidden_all = lax.all_gather(hidden, "tensor", axis=0, tiled=True)
    return jnp.dot(hidden_all, down_weight, preferred_element_type=F32)


def per_device(
    tokens,
    frozen_gate_weight,
    frozen_up_weight,
    frozen_down_weight,
    adapter_down_weight,
    adapter_up_weight,
    routes,
    route_gate_weights,
    output_gradient,
):
    n_expert = lax.axis_size("expert")
    tok_count, width_part = tokens.shape
    resident = adapter_down_weight.shape[0]
    most_slots = max(2, 4 * tok_count // (resident * n_expert))
    capacity = most_slots * n_expert
    total = tok_count * n_expert
    shard_rows = lax.all_gather(tokens, "expert", axis=0, tiled=True)
    meta = jnp.concatenate([routes.T.astype(F32), route_gate_weights.T], axis=0)
    meta_all = lax.all_gather(meta, "expert", axis=1, tiled=True)
    grad_rows = lax.all_gather(output_gradient, "expert", axis=0, tiled=True)
    local = (lax.axis_index("expert") * resident + jnp.arange(resident)).astype(F32)
    hit_0 = meta_all[0][None, :] == local[:, None]
    hit_1 = meta_all[1][None, :] == local[:, None]
    member = hit_0 | hit_1
    weight = jnp.where(hit_0, meta_all[2][None, :], 0.0) + jnp.where(
        hit_1, meta_all[3][None, :], 0.0
    )
    span = jnp.arange(tok_count)
    before = (span[:, None] < span[None, :]).astype(BF16)
    rank = jnp.dot(
        member.astype(BF16).reshape(resident * n_expert, tok_count),
        before,
        preferred_element_type=F32,
    ).reshape(resident, total)
    base_slot = (jnp.arange(total) // tok_count * most_slots).astype(F32)
    slot = jnp.where(member, rank + base_slot[None, :], -1.0)
    select = slot[:, None, :] == jnp.arange(capacity, dtype=F32)[None, :, None]
    slot_weight = jnp.sum(jnp.where(select, weight[:, None, :], 0.0), axis=2)
    pick = select.astype(BF16).reshape(resident * capacity, total)
    inputs = jnp.dot(pick, shard_rows, preferred_element_type=F32).astype(BF16)
    inputs = inputs.reshape(resident, capacity, width_part)
    cotangents = jnp.dot(pick, grad_rows, preferred_element_type=F32)
    scaled = (slot_weight[:, :, None] * cotangents.reshape(resident, capacity, width_part)).astype(
        BF16
    )
    low_part = jnp.einsum(
        "ecw,ewr->ecr", inputs, adapter_down_weight, preferred_element_type=F32
    ).astype(BF16)
    back_part = jnp.einsum(
        "ecw,erw->ecr", scaled, adapter_up_weight, preferred_element_type=F32
    ).astype(BF16)
    both = lax.psum(jnp.concatenate([low_part, back_part], axis=2), "tensor")
    rank_width = low_part.shape[2]
    low, back = (both[:, :, :rank_width], both[:, :, rank_width:])
    grad_up = jnp.einsum("ecr,ecw->erw", low, scaled, preferred_element_type=F32).astype(BF16)
    grad_down = jnp.einsum("ecw,ecr->ewr", inputs, back, preferred_element_type=F32).astype(BF16)
    rows = jnp.einsum("ecr,erw->ecw", low, adapter_up_weight, preferred_element_type=F32)
    rows = (slot_weight[:, :, None] * rows).astype(BF16).reshape(resident * capacity, width_part)
    adapter_part = lax.dot_general(pick, rows, (((0,), (0,)), ((), ())), preferred_element_type=F32)
    base_part = frozen_layer(shard_rows, frozen_gate_weight, frozen_up_weight, frozen_down_weight)
    ffn_out = lax.psum_scatter(
        (base_part + adapter_part).astype(BF16), "expert", scatter_dimension=0, tiled=True
    )
    return (ffn_out, grad_down, grad_up)


def solution(mesh):
    placed = (
        P("expert", "tensor"),
        P("tensor", "expert"),
        P("tensor", "expert"),
        P("expert", "tensor"),
        P("expert", "tensor", None),
        P("expert", None, "tensor"),
        P("expert", None),
        P("expert", None),
        P("expert", "tensor"),
    )
    return jax.shard_map(
        per_device,
        mesh=mesh,
        in_specs=placed,
        out_specs=(P("expert", "tensor"), P("expert", "tensor", None), P("expert", None, "tensor")),
        check_vma=False,
    )
```

profile of v0, /device:TPU:0, one launch (start us, length us, event | category | flops | bytes accessed | tf_op | source)
XLA Modules:
  0.0 358.7 jit_solution(514019846233866210)
XLA Ops:
  7.2 0.7 all-gather.5.cloned.1.call-update
  8.0 54.0 %all-gather.5.cloned.1.call-done = bf16[512,2048]{1,0:T(8,128)(2,1)} async-done(((bf16[64,2048]{1,0:T(8,128)(2,1)}), bf16[512,2048]{1,0:T(8,128)(2,1)}) %all-gather.5.cloned.1.call-update) | async-done | bytes 2097168 | tf_op jit(solution)/shard_map/all_gather | solution.py:43
  62.0 14.9 %convolution_convert_fusion = bf16[512,3584]{1,0:T(8,128)(2,1)} fusion(bf16[512,2048]{1,0:T(8,128)(2,1)} %all-gather.5.cloned.1.call-done, bf16[2048,3584]{1,0:T(8,128)(2,1)} %param.11), kind=kOutput, calls=%fused_computation.1 | convolution fusion | flops 7518027776 | bytes 20447232 | tf_op jit(solution)/shard_map/dot_general | solution.py:17
  76.9 12.4 %convolution_convert_fusion.1 = bf16[512,3584]{1,0:T(8,128)(2,1)} fusion(bf16[512,2048]{1,0:T(8,128)(2,1)S(1)} %copy-done.4, bf16[2048,3584]{1,0:T(8,128)(2,1)} %param.10), kind=kOutput, calls=%fused_computation.2 | convolution fusion | flops 7518027776 | bytes 20447232 | tf_op jit(solution)/shard_map/dot_general | solution.py:16
  89.3 6.9 %pad_maximum_fusion = bf16[512,7168]{1,0:T(8,128)(2,1)} fusion(bf16[512,3584]{1,0:T(8,128)(2,1)} %convolution_convert_fusion, bf16[512,3584]{1,0:T(8,128)(2,1)} %convolution_convert_fusion.1), kind=kLoop, calls=%fused_computation | loop fusion | flops 14680064 | bytes 14680064 | tf_op jit(solution)/shard_map/concatenate | solution.py:19
  96.2 0.7 all-gather.9.cloned.1.call-update
  96.9 63.8 %reduce-scatter.3.cloned.1.call-done = bf16[128,7168]{1,0:T(8,128)(2,1)} async-done(((bf16[512,7168]{1,0:T(8,128)(2,1)}), bf16[128,7168]{1,0:T(8,128)(2,1)}) %reduce-scatter.3.cloned.1.call-update) | async-done | bytes 1835024 | tf_op jit(solution)/shard_map/reduce_scatter | solution.py:18
  160.8 1.9 convert_element_type.61
  162.7 1.4 fusion.4
  164.2 26.2 %all-gather = f32[8,64,4]{1,2,0:T(4,128)S(1)} all-gather(f32[1,64,4]{1,2,0:T(4,128)S(1)} %maximum_bitcast_fusion), channel_id=1, replica_groups=mesh['expert'=8,'tensor'=4] {'expert'}, dimensions={0}, use_global_device_ids=true | all-gather | bytes 9216 | tf_op jit(solution)/shard_map/all_gather | solution.py:45
  191.6 2.3 convolution_convert_fusion.4
  193.9 18.2 %all-gather.9.cloned.1.call-done = bf16[512,2048]{1,0:T(8,128)(2,1)} async-done(((bf16[64,2048]{1,0:T(8,128)(2,1)}), bf16[512,2048]{1,0:T(8,128)(2,1)}) %all-gather.9.cloned.1.call-update) | async-done | bytes 2097168 | tf_op jit(solution)/shard_map/all_gather | solution.py:46
  212.1 2.3 fusion.1
  214.4 0.8 convolution_convert_fusion.5
  215.3 1.1 copy-done.3
  216.9 0.7 pad_maximum_fusion.1
  217.9 26.3 %all-gather.7.cloned.1.call-done = bf16[512,3584]{1,0:T(8,128)(2,1)} async-done(((bf16[128,3584]{1,0:T(8,128)(2,1)}), bf16[512,3584]{1,0:T(8,128)(2,1)}) %all-gather.7.cloned.1.call-update) | async-done | bytes 3670032 | tf_op jit(solution)/shard_map/all_gather | solution.py:22
  244.1 13.5 %fusion.24 = f32[512,2048]{1,0:T(8,128)} fusion(bf16[512,3584]{1,0:T(8,128)(2,1)} %all-gather.7.cloned.1.call-done, bf16[3584,2048]{1,0:T(8,128)(2,1)} %param.12), kind=kOutput, calls=%fused_computation.54 | convolution fusion | flops 7516192768 | bytes 22544384 | tf_op jit(solution)/shard_map/dot_general | solution.py:23
  257.6 21.1 %all-reduce.2.cloned.1.call-done = bf16[4,64,256]{2,1,0:T(8,128)(2,1)} async-done(((bf16[4,64,256]{2,1,0:T(8,128)(2,1)}), bf16[4,64,256]{2,1,0:T(8,128)(2,1)}) %all-reduce.2.cloned.1.call-update) | async-done | bytes 131088 | tf_op jit(solution)/shard_map/psum | solution.py:78
  278.7 4.6 %fusion = bf16[512,2048]{1,0:T(8,128)(2,1)} fusion(f32[512,2048]{1,0:T(8,128)} %fusion.24, bf16[4,128,2048]{2,1,0:T(8,128)(2,1)S(1)} %copy-done, f32[4,64]{1,0:T(4,128)S(1)} %select_reduce_fusion, f32[4,512]{1,0:T(4,128)S(1)} %get-tuple-element.9, bf16[4,64,256]{2,1,0:T(8,128)(2,1)} %all-reduce.2.cloned.1.call-done), kind=kOutput, calls=%fused_computation.4 | convolution fusion | flops 674365440 | bytes 8463360 | tf_op jit(solution)/shard_map/dot_general | solution.py:85
  283.3 0.9 copy-done.5
  284.2 2.2 convolution_convert_fusion.3
  286.4 2.1 convolution_convert_fusion.2
  288.5 63.4 %reduce-scatter.5.cloned.1.call-done = bf16[64,2048]{1,0:T(8,128)(2,1)} async-done(((bf16[512,2048]{1,0:T(8,128)(2,1)}), bf16[64,2048]{1,0:T(8,128)(2,1)}) %reduce-scatter.5.cloned.1.call-update) | async-done | bytes 262160 | tf_op jit(solution)/shard_map/reduce_scatter | solution.py:87
  (43 shorter events, 2.2 us)
Async XLA Ops:
  7.2 207.2 %copy-start = (bf16[4,128,2048]{2,1,0:T(8,128)(2,1)S(1)}, bf16[4,128,2048]{2,1,0:T(8,128)(2,1)}, u32[]{:S(2)}) copy-start(bf16[4,128,2048]{2,1,0:T(8,128)(2,1)} %param.14) | copy-start | bytes 6291460
  7.2 54.8 %all-gather.5.cloned.1.call-start = ((), (), s32[]{:S(2)}) async-start(), calls=%async_computation.2 | async-start | bytes 2359296 | tf_op jit(solution)/shard_map/all_gather | solution.py:43
  7.9 152.9 %reduce-scatter.3.cloned.1.call-start = ((), (), s32[]{:S(2)}) async-start(), calls=%async_computation.3 | async-start | bytes 9175040 | tf_op jit(solution)/shard_map/reduce_scatter | solution.py:18
  62.0 15.0 %copy-start.4 = (bf16[512,2048]{1,0:T(8,128)(2,1)S(1)}, bf16[512,2048]{1,0:T(8,128)(2,1)}, u32[]{:S(2)}) copy-start(bf16[512,2048]{1,0:T(8,128)(2,1)} %all-gather.5.cloned.1.call-done) | copy-start | bytes 6291460
  96.2 115.9 %all-gather.9.cloned.1.call-start = ((), (), s32[]{:S(2)}) async-start(), calls=%async_computation.5 | async-start | bytes 2359296 | tf_op jit(solution)/shard_map/all_gather | solution.py:46
  96.9 147.2 %all-gather.7.cloned.1.call-start = ((), (), s32[]{:S(2)}) async-start(), calls=%async_computation.4 | async-start | bytes 4587520 | tf_op jit(solution)/shard_map/all_gather | solution.py:22
  162.7 1.5 copy-start.6
  162.7 1.5 copy-start.7
  164.1 114.5 %all-reduce.2.cloned.1.call-start = ((), (), s32[]{:S(2)}) async-start(), calls=%async_computation.6 | async-start | bytes 262144 | tf_op jit(solution)/shard_map/psum | solution.py:78
  214.4 2.5 copy-start.1
  214.4 2.0 copy-start.3
  217.6 134.2 %reduce-scatter.5.cloned.1.call-start = ((), (), s32[]{:S(2)}) async-start(), calls=%async_computation.7 | async-start | bytes 2359296 | tf_op jit(solution)/shard_map/reduce_scatter | solution.py:87
  283.3 0.9 copy-start.5
  284.2 2.2 copy-start.2
Sparse Core Ops, SparseCore 0:
  10.1 51.7 all-gather.4
  96.3 64.4 reduce-scatter.2
  162.9 49.1 all-gather.8
  214.1 30.0 all-gather.6
  246.9 31.7 all-reduce.1
  283.4 68.3 reduce-scatter.4
where the time goes:
time: 359 us
  waiting for transfers between devices  248 us (69%)
  matrix products  55.8 us (16%)
  blocking collectives  26.2 us (7%)
  between operations  14.3 us (4%)
  other arithmetic  11.2 us (3%)
    reduce_scatter x1, waiting for transfers between devices, frozen_layer(): lax.psum_scatter(jnp.concatenate([gate_part, up_part], axis=1), 'tensor',...  63.8 us
    reduce_scatter x1, waiting for transfers between devices, per_device(): lax.psum_scatter((base_part + adapter_part).astype(BF16), 'expert', scatt...  63.4 us
    all_gather x1, waiting for transfers between devices, per_device(): shard_rows = lax.all_gather(tokens, 'expert', axis=0, tiled=True)  54 us
    all_gather x1, waiting for transfers between devices, frozen_layer(): hidden_all = lax.all_gather(hidden, 'tensor', axis=0, tiled=True)  26.3 us
    all_gather x1, blocking collectives, per_device(): meta_all = lax.all_gather(meta, 'expert', axis=1, tiled=True)  26.2 us
    psum x1, waiting for transfers between devices, per_device(): both = lax.psum(jnp.concatenate([low_part, back_part], axis=2), 'tensor')  21.1 us
    all_gather x1, waiting for transfers between devices, per_device(): grad_rows = lax.all_gather(output_gradient, 'expert', axis=0, tiled=True)  18.2 us
    dot_general x1, matrix products, frozen_layer(): jnp.dot(shard_rows, up_weight, preferred_element_type=F32).astype(BF16)  14.9 us
  transfers between devices with their start and end apart: 6, of which 6 were waited for; matrix products, arithmetic and copies ran while one was open for 8% of the time, Pallas kernels for 0%

commit v1 on v0

--- a/solution.py
+++ b/solution.py
@@ -5,6 +5,18 @@
 
 F32 = jnp.float32
 BF16 = jnp.bfloat16
+
+
+def ring_gather(shard, axis, dim):
+    ways, here, turn = (lax.axis_size(axis), lax.axis_index(axis), shard.shape[dim])
+    dims = [n * ways if d == dim else n for d, n in enumerate(shard.shape)]
+    full = lax.dynamic_update_slice_in_dim(
+        jnp.zeros(dims, shard.dtype), shard, here * turn, axis=dim
+    )
+    for far in range(1, ways):
+        shard = lax.ppermute(shard, axis, [(d, (d + 1) % ways) for d in range(ways)])
+        full = lax.dynamic_update_slice_in_dim(full, shard, (here - far) % ways * turn, axis=dim)
+    return full
 
 
 def activate(gate_part, up_part):
@@ -42,7 +54,7 @@
     total = tok_count * n_expert
     shard_rows = lax.all_gather(tokens, "expert", axis=0, tiled=True)
     meta = jnp.concatenate([routes.T.astype(F32), route_gate_weights.T], axis=0)
-    meta_all = lax.all_gather(meta, "expert", axis=1, tiled=True)
+    meta_all = ring_gather(meta, "expert", 1)
     grad_rows = lax.all_gather(output_gradient, "expert", axis=0, tiled=True)
     local = (lax.axis_index("expert") * resident + jnp.arange(resident)).astype(F32)
     hit_0 = meta_all[0][None, :] == local[:, None]

time: 359 us -> 359 us (level)
  blocking collectives: 26.2 us -> 0 us
  waiting for transfers between devices: 248 us -> 272 us
    ppermute x0 -> x7, waiting for transfers between devices: none -> 41.1 us  [ring_gather(): lax.ppermute(shard, axis, [(d, (d + 1) % ways) for d in range(ways)])]
    all_gather x1 -> x0, blocking collectives: 26.2 us -> none  [per_device(): meta_all = lax.all_gather(meta, 'expert', axis=1, tiled=True)]
    all_gather x1, waiting for transfers between devices: 18.2 us -> 0.67 us  [per_device(): grad_rows = lax.all_gather(output_gradient, 'expert', axis=0, tiled=True)]
  transfers between devices with their start and end apart: 6 -> 13, of which waited for: 6 -> 13; matrix products, arithmetic and copies ran while one was open for 8% -> 8% of each run, Pallas kernels for 0% -> 0%
where the time goes in v1:
time: 359 us
  waiting for transfers between devices  272 us (76%)
  matrix products  55.8 us (16%)
  between operations  14.3 us (4%)
  other arithmetic  11.2 us (3%)
  local copies, waits for them, and re-layouts  4.03 us (1%)
    reduce_scatter x1, waiting for transfers between devices, frozen_layer(): lax.psum_scatter(jnp.concatenate([gate_part, up_part], axis=1), 'tensor',...  63.9 us
    reduce_scatter x1, waiting for transfers between devices, per_device(): lax.psum_scatter((base_part + adapter_part).astype(BF16), 'expert', scatt...  63.5 us
    all_gather x1, waiting for transfers between devices, per_device(): shard_rows = lax.all_gather(tokens, 'expert', axis=0, tiled=True)  54 us
    ppermute x7, waiting for transfers between devices, ring_gather(): lax.ppermute(shard, axis, [(d, (d + 1) % ways) for d in range(ways)])  41.1 us
    all_gather x1, waiting for transfers between devices, frozen_layer(): hidden_all = lax.all_gather(hidden, 'tensor', axis=0, tiled=True)  26.3 us
    psum x1, waiting for transfers between devices, per_device(): both = lax.psum(jnp.concatenate([low_part, back_part], axis=2), 'tensor')  21.1 us
    dot_general x1, matrix products, frozen_layer(): jnp.dot(shard_rows, up_weight, preferred_element_type=F32).astype(BF16)  15 us
    dot_general x1, matrix products, frozen_layer(): return jnp.dot(hidden_all, down_weight, preferred_element_type=F32)  13.4 us
  transfers between devices with their start and end apart: 13, of which 13 were waited for; matrix products, arithmetic and copies ran while one was open for 8% of the time, Pallas kernels for 0%

profile of v1, /device:TPU:0, one launch (start us, length us, event | category | flops | bytes accessed | tf_op | source)
XLA Modules:
  0.0 359.2 jit_solution(4823874996972786184)
XLA Ops:
  8.0 54.0 %all-gather.4.cloned.1.call-done = bf16[512,2048]{1,0:T(8,128)(2,1)} async-done(((bf16[64,2048]{1,0:T(8,128)(2,1)}), bf16[512,2048]{1,0:T(8,128)(2,1)}) %all-gather.4.cloned.1.call-update) | async-done | bytes 2097168 | tf_op jit(solution)/shard_map/all_gather | solution.py:55
  62.0 15.0 %convolution_convert_fusion = bf16[512,3584]{1,0:T(8,128)(2,1)} fusion(bf16[512,2048]{1,0:T(8,128)(2,1)} %all-gather.4.cloned.1.call-done, bf16[2048,3584]{1,0:T(8,128)(2,1)} %param.11), kind=kOutput, calls=%fused_computation.1 | convolution fusion | flops 7518027776 | bytes 20447232 | tf_op jit(solution)/shard_map/dot_general | solution.py:29
  76.9 12.4 %convolution_convert_fusion.1 = bf16[512,3584]{1,0:T(8,128)(2,1)} fusion(bf16[512,2048]{1,0:T(8,128)(2,1)S(1)} %copy-done.4, bf16[2048,3584]{1,0:T(8,128)(2,1)} %param.10), kind=kOutput, calls=%fused_computation.2 | convolution fusion | flops 7518027776 | bytes 20447232 | tf_op jit(solution)/shard_map/dot_general | solution.py:28
  89.3 6.9 %pad_maximum_fusion = bf16[512,7168]{1,0:T(8,128)(2,1)} fusion(bf16[512,3584]{1,0:T(8,128)(2,1)} %convolution_convert_fusion, bf16[512,3584]{1,0:T(8,128)(2,1)} %convolution_convert_fusion.1), kind=kLoop, calls=%fused_computation | loop fusion | flops 14680064 | bytes 14680064 | tf_op jit(solution)/shard_map/concatenate | solution.py:31
  97.0 63.9 %reduce-scatter.3.cloned.1.call-done = bf16[128,7168]{1,0:T(8,128)(2,1)} async-done(((bf16[512,7168]{1,0:T(8,128)(2,1)}), bf16[128,7168]{1,0:T(8,128)(2,1)}) %reduce-scatter.3.cloned.1.call-update) | async-done | bytes 1835024 | tf_op jit(solution)/shard_map/reduce_scatter | solution.py:30
  160.9 1.9 convert_element_type.61
  162.7 1.4 fusion.4
  164.3 1.5 collective-permute-start
  165.8 4.8 %collective-permute-done = f32[4,64]{1,0:T(4,128)S(1)} collective-permute-done((f32[4,64]{1,0:T(4,128)S(1)}, f32[4,64]{1,0:T(4,128)S(1)}, u32[]{:S(2)}, u32[]{:S(2)}) %collective-permute-start) | collective-permute-done | bytes 1056 | tf_op jit(solution)/shard_map/ppermute | solution.py:17
  170.6 6.3 %collective-permute-done.1 = f32[4,64]{1,0:T(4,128)S(1)} collective-permute-done((f32[4,64]{1,0:T(4,128)S(1)}, f32[4,64]{1,0:T(4,128)S(1)}, u32[]{:S(2)}, u32[]{:S(2)}) %collective-permute-start.1) | collective-permute-done | bytes 1056 | tf_op jit(solution)/shard_map/ppermute | solution.py:17
  176.9 6.3 %collective-permute-done.2 = f32[4,64]{1,0:T(4,128)S(1)} collective-permute-done((f32[4,64]{1,0:T(4,128)S(1)}, f32[4,64]{1,0:T(4,128)S(1)}, u32[]{:S(2)}, u32[]{:S(2)}) %collective-permute-start.2) | collective-permute-done | bytes 1056 | tf_op jit(solution)/shard_map/ppermute | solution.py:17
  183.2 6.3 %collective-permute-done.3 = f32[4,64]{1,0:T(4,128)S(1)} collective-permute-done((f32[4,64]{1,0:T(4,128)S(1)}, f32[4,64]{1,0:T(4,128)S(1)}, u32[]{:S(2)}, u32[]{:S(2)}) %collective-permute-start.3) | collective-permute-done | bytes 1056 | tf_op jit(solution)/shard_map/ppermute | solution.py:17
  189.5 6.3 %collective-permute-done.4 = f32[4,64]{1,0:T(4,128)S(1)} collective-permute-done((f32[4,64]{1,0:T(4,128)S(1)}, f32[4,64]{1,0:T(4,128)S(1)}, u32[]{:S(2)}, u32[]{:S(2)}) %collective-permute-start.4) | collective-permute-done | bytes 1056 | tf_op jit(solution)/shard_map/ppermute | solution.py:17
  195.8 6.5 %collective-permute-done.5 = f32[4,64]{1,0:T(4,128)S(1)} collective-permute-done((f32[4,64]{1,0:T(4,128)S(1)}, f32[4,64]{1,0:T(4,128)S(1)}, u32[]{:S(2)}, u32[]{:S(2)}) %collective-permute-start.5) | collective-permute-done | bytes 1056 | tf_op jit(solution)/shard_map/ppermute | solution.py:17
  203.9 4.7 %collective-permute-done.6 = f32[4,64]{1,0:T(4,128)S(1)} collective-permute-done((f32[4,64]{1,0:T(4,128)S(1)}, f32[4,64]{1,0:T(4,128)S(1)}, u32[]{:S(2)}, u32[]{:S(2)}) %collective-permute-start.6) | collective-permute-done | bytes 1056 | tf_op jit(solution)/shard_map/ppermute | solution.py:17
  209.6 2.3 convolution_convert_fusion.4
  212.6 2.3 fusion.1
  218.1 26.3 %all-gather.6.cloned.1.call-done = bf16[512,3584]{1,0:T(8,128)(2,1)} async-done(((bf16[128,3584]{1,0:T(8,128)(2,1)}), bf16[512,3584]{1,0:T(8,128)(2,1)}) %all-gather.6.cloned.1.call-update) | async-done | bytes 3670032 | tf_op jit(solution)/shard_map/all_gather | solution.py:34
  244.5 13.4 %fusion.24 = f32[512,2048]{1,0:T(8,128)} fusion(bf16[512,3584]{1,0:T(8,128)(2,1)} %all-gather.6.cloned.1.call-done, bf16[3584,2048]{1,0:T(8,128)(2,1)} %param.12), kind=kOutput, calls=%fused_computation.54 | convolution fusion | flops 7516192768 | bytes 22544384 | tf_op jit(solution)/shard_map/dot_general | solution.py:35
  257.9 21.1 %all-reduce.2.cloned.1.call-done = bf16[4,64,256]{2,1,0:T(8,128)(2,1)} async-done(((bf16[4,64,256]{2,1,0:T(8,128)(2,1)}), bf16[4,64,256]{2,1,0:T(8,128)(2,1)}) %all-reduce.2.cloned.1.call-update) | async-done | bytes 131088 | tf_op jit(solution)/shard_map/psum | solution.py:90
  279.0 4.7 %fusion = bf16[512,2048]{1,0:T(8,128)(2,1)} fusion(f32[512,2048]{1,0:T(8,128)} %fusion.24, bf16[4,128,2048]{2,1,0:T(8,128)(2,1)S(1)} %copy-done, f32[4,64]{1,0:T(4,128)S(1)} %select_reduce_fusion, f32[4,512]{1,0:T(4,128)S(1)} %get-tuple-element.9, bf16[4,64,256]{2,1,0:T(8,128)(2,1)} %all-reduce.2.cloned.1.call-done), kind=kOutput, calls=%fused_computation.4 | convolution fusion | flops 674365440 | bytes 8463360 | tf_op jit(solution)/shard_map/dot_general | solution.py:97
  284.6 2.2 convolution_convert_fusion.3
  286.8 2.1 convolution_convert_fusion.2
  288.8 63.5 %reduce-scatter.5.cloned.1.call-done = bf16[64,2048]{1,0:T(8,128)(2,1)} async-done(((bf16[512,2048]{1,0:T(8,128)(2,1)}), bf16[64,2048]{1,0:T(8,128)(2,1)}) %reduce-scatter.5.cloned.1.call-update) | async-done | bytes 262160 | tf_op jit(solution)/shard_map/reduce_scatter | solution.py:99
  (63 shorter events, 9.0 us)
Async XLA Ops:
  7.2 207.7 %copy-start = (bf16[4,128,2048]{2,1,0:T(8,128)(2,1)S(1)}, bf16[4,128,2048]{2,1,0:T(8,128)(2,1)}, u32[]{:S(2)}) copy-start(bf16[4,128,2048]{2,1,0:T(8,128)(2,1)} %param.14) | copy-start | bytes 6291460
  7.2 54.8 %all-gather.4.cloned.1.call-start = ((), (), s32[]{:S(2)}) async-start(), calls=%async_computation.2 | async-start | bytes 2359296 | tf_op jit(solution)/shard_map/all_gather | solution.py:55
  7.9 152.9 %reduce-scatter.3.cloned.1.call-start = ((), (), s32[]{:S(2)}) async-start(), calls=%async_computation.3 | async-start | bytes 9175040 | tf_op jit(solution)/shard_map/reduce_scatter | solution.py:30
  62.0 15.0 %copy-start.4 = (bf16[512,2048]{1,0:T(8,128)(2,1)S(1)}, bf16[512,2048]{1,0:T(8,128)(2,1)}, u32[]{:S(2)}) copy-start(bf16[512,2048]{1,0:T(8,128)(2,1)} %all-gather.4.cloned.1.call-done) | copy-start | bytes 6291460
  96.2 116.4 %all-gather.8.cloned.1.call-start = ((), (), s32[]{:S(2)}) async-start(), calls=%async_computation.5 | async-start | bytes 2359296 | tf_op jit(solution)/shard_map/all_gather | solution.py:58
  96.9 147.5 %all-gather.6.cloned.1.call-start = ((), (), s32[]{:S(2)}) async-start(), calls=%async_computation.4 | async-start | bytes 4587520 | tf_op jit(solution)/shard_map/all_gather | solution.py:34
  162.7 1.5 copy-start.6
  162.7 1.5 copy-start.7
  164.2 114.8 %all-reduce.2.cloned.1.call-start = ((), (), s32[]{:S(2)}) async-start(), calls=%async_computation.6 | async-start | bytes 262144 | tf_op jit(solution)/shard_map/psum | solution.py:90
  164.3 6.3 %collective-permute-start = (f32[4,64]{1,0:T(4,128)S(1)}, f32[4,64]{1,0:T(4,128)S(1)}, u32[]{:S(2)}, u32[]{:S(2)}) collective-permute-start(f32[4,64]{1,0:T(4,128)S(1)} %pad_maximum_fusion.2), channel_id=1, source_target_pairs={{0,4},{4,8},{8,12},{12,16},{16,20},{20,24},{24,28},{28,0},{1,5},{5... | collective-permute-start | bytes 3080 | tf_op jit(solution)/shard_map/ppermute | solution.py:17
  170.6 6.3 %collective-permute-start.1 = (f32[4,64]{1,0:T(4,128)S(1)}, f32[4,64]{1,0:T(4,128)S(1)}, u32[]{:S(2)}, u32[]{:S(2)}) collective-permute-start(f32[4,64]{1,0:T(4,128)S(1)} %collective-permute-done), channel_id=1, source_target_pairs={{0,4},{4,8},{8,12},{12,16},{16,20},{20,24},{24,28},{28,0},{1,5},{5... | collective-permute-start | bytes 3080 | tf_op jit(solution)/shard_map/ppermute | solution.py:17
  176.9 6.3 %collective-permute-start.2 = (f32[4,64]{1,0:T(4,128)S(1)}, f32[4,64]{1,0:T(4,128)S(1)}, u32[]{:S(2)}, u32[]{:S(2)}) collective-permute-start(f32[4,64]{1,0:T(4,128)S(1)} %collective-permute-done.1), channel_id=1, source_target_pairs={{0,4},{4,8},{8,12},{12,16},{16,20},{20,24},{24,28},{28,0},{1,5},{5... | collective-permute-start | bytes 3080 | tf_op jit(solution)/shard_map/ppermute | solution.py:17
  183.2 6.3 %collective-permute-start.3 = (f32[4,64]{1,0:T(4,128)S(1)}, f32[4,64]{1,0:T(4,128)S(1)}, u32[]{:S(2)}, u32[]{:S(2)}) collective-permute-start(f32[4,64]{1,0:T(4,128)S(1)} %collective-permute-done.2), channel_id=1, source_target_pairs={{0,4},{4,8},{8,12},{12,16},{16,20},{20,24},{24,28},{28,0},{1,5},{5... | collective-permute-start | bytes 3080 | tf_op jit(solution)/shard_map/ppermute | solution.py:17
  189.5 6.3 %collective-permute-start.4 = (f32[4,64]{1,0:T(4,128)S(1)}, f32[4,64]{1,0:T(4,128)S(1)}, u32[]{:S(2)}, u32[]{:S(2)}) collective-permute-start(f32[4,64]{1,0:T(4,128)S(1)} %collective-permute-done.3), channel_id=1, source_target_pairs={{0,4},{4,8},{8,12},{12,16},{16,20},{20,24},{24,28},{28,0},{1,5},{5... | collective-permute-start | bytes 3080 | tf_op jit(solution)/shard_map/ppermute | solution.py:17
  195.8 6.5 %collective-permute-start.5 = (f32[4,64]{1,0:T(4,128)S(1)}, f32[4,64]{1,0:T(4,128)S(1)}, u32[]{:S(2)}, u32[]{:S(2)}) collective-permute-start(f32[4,64]{1,0:T(4,128)S(1)} %collective-permute-done.4), channel_id=1, source_target_pairs={{0,4},{4,8},{8,12},{12,16},{16,20},{20,24},{24,28},{28,0},{1,5},{5... | collective-permute-start | bytes 3080 | tf_op jit(solution)/shard_map/ppermute | solution.py:17
  202.2 6.3 %collective-permute-start.6 = (f32[4,64]{1,0:T(4,128)S(1)}, f32[4,64]{1,0:T(4,128)S(1)}, u32[]{:S(2)}, u32[]{:S(2)}) collective-permute-start(f32[4,64]{1,0:T(4,128)S(1)} %collective-permute-done.5), channel_id=1, source_target_pairs={{0,4},{4,8},{8,12},{12,16},{16,20},{20,24},{24,28},{28,0},{1,5},{5... | collective-permute-start | bytes 3080 | tf_op jit(solution)/shard_map/ppermute | solution.py:17
  214.9 2.5 copy-start.1
  214.9 2.0 copy-start.3
  218.1 134.2 %reduce-scatter.5.cloned.1.call-start = ((), (), s32[]{:S(2)}) async-start(), calls=%async_computation.7 | async-start | bytes 2359296 | tf_op jit(solution)/shard_map/reduce_scatter | solution.py:99
  283.6 0.9 copy-start.5
  284.6 2.2 copy-start.2
Sparse Core Ops, SparseCore 0:
  10.1 51.7 all-gather.3
  96.3 64.4 reduce-scatter.2
  163.0 49.5 all-gather.7
  214.5 29.8 all-gather.5
  247.2 31.7 all-reduce.1
  283.8 68.4 reduce-scatter.4
